TPU v7x, 32 devices: a whole 2x2x4 slice. The times are simulated.
32 devices in a mesh: tm: 4 (over y, x), stn: 8 (over z, core).
Axes of the slice: x: 2, y: 2, z: 4, core: 2. Of those that a mesh axis runs over, the one named last changes fastest.
Arguments:
- voltages: bfloat16 [2, 1024, 16384], P(None, 'stn', 'tm'), may hold values from -6 to 6
- filter_taps: float32 [12, 4096], replicated, may hold values from -1.75 to 1.75
- beam_weights: int32 [2, 512, 1024], P(None, 'stn'), may hold values from -32768 to 32767
- station_map: int32 [512], replicated, may hold values from 0 to 511, each once
- station_flags: int32 [512], replicated, may hold values 0 or 1
Outputs:
- beam_power: float32 [512, 4, 4096], P('stn', 'tm')
Inputs may be any that keep to these rules, and one draw needn't show every extreme that they name: `station_map`: each station number appears once.
All inputs are finite; a program needn't handle non-finite values.
Results may differ from a plain program's by a relative error of at most 0.0039.
Values may be sent and summed in bfloat16 or wider, within the bound.
A program may use at most 64 MiB of HBM per device.

v0:
```python
import math

import jax
import jax.numpy as jnp
from jax import lax
from jax.sharding import PartitionSpec as P

RADIX = 64


exact_mode = lax.Precision.HIGHEST


def transform(real_in, imag_in, channels):
    index_row = jnp.arange(RADIX, dtype=jnp.int32)
    product = index_row[:, None] * index_row[None, :]
    angle_table = (product % RADIX).astype(jnp.float32) * (2.0 * math.pi / RADIX)
    cosine = jnp.cos(angle_table)
    sine_part = jnp.sin(angle_table)
    twiddle = product.astype(jnp.float32) * (2.0 * math.pi / channels)
    twiddle_cos = jnp.cos(twiddle)
    twiddle_sin = jnp.sin(twiddle)
    batch_rows = real_in.shape[0]
    real_cube = real_in.reshape(batch_rows, RADIX, RADIX)
    imag_cube = imag_in.reshape(batch_rows, RADIX, RADIX)
    mid_real = jnp.einsum("pab,ak->pbk", real_cube, cosine, precision=exact_mode) + jnp.einsum(
        "pab,ak->pbk", imag_cube, sine_part, precision=exact_mode
    )
    mid_imag = jnp.einsum("pab,ak->pbk", imag_cube, cosine, precision=exact_mode) - jnp.einsum(
        "pab,ak->pbk", real_cube, sine_part, precision=exact_mode
    )
    turn_real = mid_real * twiddle_cos + mid_imag * twiddle_sin
    turn_imag = mid_imag * twiddle_cos - mid_real * twiddle_sin
    out_real = jnp.einsum("pbk,bm->pmk", turn_real, cosine, precision=exact_mode) + jnp.einsum(
        "pbk,bm->pmk", turn_imag, sine_part, precision=exact_mode
    )
    out_imag = jnp.einsum("pbk,bm->pmk", turn_imag, cosine, precision=exact_mode) - jnp.einsum(
        "pbk,bm->pmk", turn_real, sine_part, precision=exact_mode
    )
    norm_scale = 1.0 / math.sqrt(channels)
    return (
        out_real.reshape(batch_rows, channels) * norm_scale,
        out_imag.reshape(batch_rows, channels) * norm_scale,
    )


def filter_spectra(extended, filter_taps, frame_count):
    inputs_here = extended.shape[1]
    channels = extended.shape[3]
    filtered = jnp.zeros((2, inputs_here, frame_count, channels), jnp.float32)
    for tap_index in range(filter_taps.shape[0]):
        filtered = filtered + filter_taps[tap_index] * extended[
            :, :, tap_index : tap_index + frame_count
        ].astype(jnp.float32)
    chan_real, chan_imag = transform(
        filtered[0].reshape(-1, channels), filtered[1].reshape(-1, channels), channels
    )
    return jnp.stack([chan_real.astype(jnp.bfloat16), chan_imag.astype(jnp.bfloat16)]).reshape(
        2, inputs_here, frame_count, channels
    )


def on_device(voltages, filter_taps, beam_weights, station_map, station_flags):
    local_inputs = voltages.shape[1]
    local_stations = local_inputs // 2
    stations = station_map.shape[0]
    channels = filter_taps.shape[1]
    history = filter_taps.shape[0] - 1
    first_slot = lax.axis_index("stn") * local_stations
    slot_ids = lax.dynamic_slice_in_dim(station_map, first_slot, local_stations)
    matches = slot_ids[:, None] == jnp.arange(stations, dtype=jnp.int32)[None, :]
    flag_slot = jnp.sum(jnp.where(matches, station_flags[None, :], 0), axis=1)
    keep_mask = jnp.repeat(flag_slot, 2).astype(jnp.bfloat16)
    masked = voltages * keep_mask[None, :, None]
    weight_int = beam_weights.reshape(2, beam_weights.shape[1], stations, 2)
    weight_int = jnp.take(weight_int, station_map, axis=2).reshape(
        2, beam_weights.shape[1], 2 * stations
    )
    weight_low = (weight_int.astype(jnp.float32) * (1.0 / 32768.0)).astype(jnp.bfloat16)
    weight_all = lax.all_gather(weight_low, "stn", axis=1, tiled=True)
    inputs_all = weight_all.shape[2]
    retiled = lax.all_to_all(masked, "tm", split_axis=1, concat_axis=2, tiled=True)
    few_inputs = retiled.shape[1]
    all_frames = retiled.shape[2] // channels
    frames = retiled.reshape(2, few_inputs, all_frames, channels)
    extended = jnp.concatenate(
        [jnp.zeros((2, few_inputs, history, channels), frames.dtype), frames], axis=2
    )
    spectra = filter_spectra(extended, filter_taps, all_frames)
    turned = lax.all_to_all(
        lax.all_to_all(spectra, "tm", split_axis=2, concat_axis=1, tiled=True),
        "stn",
        split_axis=3,
        concat_axis=1,
        tiled=True,
    )
    items = turned.shape[2]
    width = turned.shape[3]
    flat_real = turned[0].reshape(inputs_all, items * width)
    flat_imag = turned[1].reshape(inputs_all, items * width)
    beam_real = jnp.dot(weight_all[0], flat_real, preferred_element_type=jnp.float32) - jnp.dot(
        weight_all[1], flat_imag, preferred_element_type=jnp.float32
    )
    beam_imag = jnp.dot(weight_all[0], flat_imag, preferred_element_type=jnp.float32) + jnp.dot(
        weight_all[1], flat_real, preferred_element_type=jnp.float32
    )
    detected = (beam_real * beam_real + beam_imag * beam_imag) / inputs_all
    channel_power = detected.reshape(-1, items, width)
    return lax.all_to_all(channel_power, "stn", split_axis=0, concat_axis=2, tiled=True)


def solution(mesh):
    placed = (P(None, "stn", "tm"), P(), P(None, "stn", None), P(), P())
    return jax.shard_map(
        on_device, mesh=mesh, in_specs=placed, out_specs=P("stn", "tm", None), check_vma=False
    )
```

profile of v0, /device:TPU:0, one launch (start us, length us, event | category | flops | bytes accessed | tf_op | source)
XLA Modules:
  0.0 256.1 jit_solution(5420655139441856221)
XLA Ops:
  8.4 5.4 %copy_multiply_fusion = bf16[2,128,4096]{2,0,1:T(2,128)(2,1)} fusion(bf16[2,128,4096]{2,1,0:T(8,128)(2,1)} %param.5, bf16[128]{0:T(256)(128)(2,1)S(1)} %convert_element_type.109), kind=kLoop, calls=%fused_computation.7 | loop fusion | flops 1048576 | bytes 4194560 | tf_op jit(solution)/shard_map/mul | solution.py:74
  13.8 5.8 %all-to-all-start = ((bf16[2,128,4096]{2,0,1:T(2,128)(2,1)}), bf16[2,128,4096]{2,0,1:T(2,128)(2,1)S(1)}, u32[]{:S(2)}, u32[]{:S(2)}) async-start(bf16[2,128,4096]{2,0,1:T(2,128)(2,1)} %copy_multiply_fusion), calls=%async_computation | async-start | bytes 4194304 | tf_op jit(solution)/shard_map/all_to_all | solution.py:82
  20.2 24.3 %all-to-all-done = bf16[2,128,4096]{2,0,1:T(2,128)(2,1)S(1)} async-done(((bf16[2,128,4096]{2,0,1:T(2,128)(2,1)}), bf16[2,128,4096]{2,0,1:T(2,128)(2,1)S(1)}, u32[]{:S(2)}, u32[]{:S(2)}) %all-to-all-start) | async-done | bytes 2097184 | tf_op jit(solution)/shard_map/all_to_all | solution.py:82
  46.4 4.6 %multiply_add_fusion = f32[2,32,4,4096]{3,2,1,0:T(4,128)S(1)} fusion(bf16[2,32,4,4096]{3,2,1,0:T(4,128)(2,1)S(1)} %bitcast.73, f32[4096]{0:T(1024)S(1)} %bitcast.86, f32[4096]{0:T(1024)S(1)} %bitcast.87, f32[4096]{0:T(1024)S(1)} %bitcast.85, f32[4096]{0:T(1024)S(1)} %bitcast.84, f32[4096]{0:T(1024)S(1)} %bitcast.83), kind=kLoop, calls=%fused_computation.4 | loop fusion | flops 12582912 | bytes 6373376 | tf_op jit(solution)/shard_map/add | solution.py:52
  52.8 3.3 %reshape_reshape_squeeze.6 = f32[128,64,64]{2,1,0:T(8,128)} reshape(f32[1,32,4,4096]{3,2,1,0:T(4,128)S(1)} %get-tuple-element.8) | data formatting | bytes 4194304 | tf_op jit(solution)/shard_map/reshape;reshape;squeeze | solution.py:24
  56.1 4.5 %copy.119 = f32[128,64,64]{0,1,2:T(8,128)S(1)} copy(f32[128,64,64]{2,1,0:T(8,128)} %reshape_reshape_squeeze.6) | data formatting | bytes 4194304 | tf_op jit(solution)/shard_map/reshape;reshape;squeeze | solution.py:24
  60.6 3.4 %fusion.36 = f32[128,64,64]{0,2,1:T(8,128)} fusion(f32[128,64,64]{0,1,2:T(8,128)S(1)} %copy.119), kind=kOutput, calls=%fused_computation.52 | convolution fusion | flops 402710528 | bytes 4194304 | tf_op jit(solution)/shard_map/pab,ak->pbk/dot_general | solution.py:26
  64.0 5.1 %reshape_reshape_squeeze.7 = f32[128,64,64]{2,1,0:T(8,128)} reshape(f32[1,32,4,4096]{3,2,1,0:T(4,128)} %get-tuple-element.7) | data formatting | bytes 4194304 | tf_op jit(solution)/shard_map/reshape;reshape;squeeze | solution.py:25
  69.1 5.5 %copy.120 = f32[128,64,64]{0,1,2:T(8,128)} copy(f32[128,64,64]{2,1,0:T(8,128)} %reshape_reshape_squeeze.7) | data formatting | bytes 4194304 | tf_op jit(solution)/shard_map/reshape;reshape;squeeze | solution.py:25
  74.6 3.9 %fusion.34 = f32[128,64,64]{0,2,1:T(8,128)S(1)} fusion(f32[128,64,64]{0,1,2:T(8,128)} %copy.120), kind=kOutput, calls=%fused_computation.50 | convolution fusion | flops 402710528 | bytes 4194304 | tf_op jit(solution)/shard_map/pab,ak->pbk/dot_general | solution.py:29
  80.7 3.3 %multiply_add_fusion.1 = (f32[128,64,64]{0,2,1:T(8,128)S(1)}, f32[128,64,64]{0,2,1:T(8,128)S(1)}) fusion(f32[128,64,64]{0,2,1:T(8,128)S(1)} %convolution_add_fusion, f32[64,64]{1,0:T(8,128)S(1)} %copy.124, f32[64,64]{1,0:T(8,128)S(1)} %copy.121, f32[128,64,64]{0,2,1:T(8,128)S(1)} %fusion.34, f32[128,64,64]{0,1,2:T(8,128)S(1)} %copy.119), kind=kOutput, calls=%fused_computation.11 | convolution fusion | flops 406380544 | bytes 10518528 | tf_op jit(solution)/shard_map/pab,ak->pbk/dot_general | solution.py:29
  87.2 4.7 %fusion = f32[64,128,64]{1,0,2:T(8,128)} fusion(f32[128,64,64]{0,2,1:T(8,128)S(1)} %get-tuple-element.6), kind=kOutput, calls=%fused_computation.12 | convolution fusion | flops 402710528 | bytes 4194304 | tf_op jit(solution)/shard_map/pbk,bm->pmk/dot_general | solution.py:37
  91.8 3.2 %fusion.12 = bf16[128,64,64]{0,1,2:T(8,128)(2,1)S(1)} fusion(f32[64,128,64]{1,0,2:T(8,128)S(1)} %fusion.2, f32[128,64,64]{0,2,1:T(8,128)S(1)} %get-tuple-element.5), kind=kOutput, calls=%fused_computation.22 | convolution fusion | flops 404283392 | bytes 5242880 | tf_op jit(solution)/shard_map/pbk,bm->pmk/dot_general | solution.py:34
  95.1 4.5 %copy.127 = bf16[128,64,64]{2,1,0:T(8,128)(2,1)} copy(bf16[128,64,64]{0,1,2:T(8,128)(2,1)S(1)} %fusion.12) | data formatting | bytes 2097152 | tf_op jit(solution)/shard_map/convert_element_type | solution.py:58
  99.6 4.6 %convert_element_type.117 = bf16[1,32,4,4096]{3,2,1,0:T(4,128)(2,1)} reshape(bf16[128,64,64]{2,1,0:T(8,128)(2,1)} %copy.127) | data formatting | bytes 2097152 | tf_op jit(solution)/shard_map/convert_element_type | solution.py:58
  104.2 4.7 %fusion.15 = bf16[128,64,64]{0,1,2:T(8,128)(2,1)S(1)} fusion(f32[64,128,64]{1,0,2:T(8,128)} %fusion, f32[128,64,64]{0,2,1:T(8,128)S(1)} %copy-done.2), kind=kOutput, calls=%fused_computation.23 | convolution fusion | flops 404283392 | bytes 5242880 | tf_op jit(solution)/shard_map/pbk,bm->pmk/dot_general | solution.py:37
  108.9 3.5 %copy.130 = bf16[128,64,64]{2,1,0:T(8,128)(2,1)S(1)} copy(bf16[128,64,64]{0,1,2:T(8,128)(2,1)S(1)} %fusion.15) | data formatting | bytes 2097152 | tf_op jit(solution)/shard_map/convert_element_type | solution.py:58
  120.3 4.6 %all-to-all-start.1 = ((bf16[2,32,4,4096]{3,1,0,2:T(8,128)(2,1)}), bf16[2,32,4,4096]{3,1,0,2:T(8,128)(2,1)}, u32[]{:S(2)}, u32[]{:S(2)}) async-start(bf16[2,32,4,4096]{3,1,0,2:T(8,128)(2,1)} %copy.131), calls=%async_computation.1 | async-start | bytes 4194304 | tf_op jit(solution)/shard_map/all_to_all | solution.py:91
  130.2 19.1 %all-to-all-done.1 = bf16[2,32,4,4096]{3,1,0,2:T(8,128)(2,1)} async-done(((bf16[2,32,4,4096]{3,1,0,2:T(8,128)(2,1)}), bf16[2,32,4,4096]{3,1,0,2:T(8,128)(2,1)}, u32[]{:S(2)}, u32[]{:S(2)}) %all-to-all-start.1) | async-done | bytes 2097184 | tf_op jit(solution)/shard_map/all_to_all | solution.py:91
  151.2 3.8 %copy.133 = bf16[2,128,1,4096]{1,0,2,3:T(2,128)(2,1)} copy(bf16[2,128,1,4096]{3,1,0,2:T(8,128)(2,1)S(1)} %bitcast.76) | data formatting | bytes 4194304 | tf_op jit(solution)/shard_map/all_to_all | solution.py:91
  154.9 5.2 %all-to-all-start.2 = ((bf16[2,128,1,4096]{1,0,2,3:T(2,128)(2,1)}), bf16[2,128,1,4096]{1,0,2,3:T(2,128)(2,1)S(1)}, u32[]{:S(2)}, u32[]{:S(2)}) async-start(bf16[2,128,1,4096]{1,0,2,3:T(2,128)(2,1)} %copy.133), calls=%async_computation.2 | async-start | bytes 4194304 | tf_op jit(solution)/shard_map/all_to_all | solution.py:90
  161.3 7.0 %fusion.86 = (bf16[1,512,1024]{2,0,1:T(2,128)(2,1)}, bf16[1,512,1024]{2,0,1:T(2,128)(2,1)}) fusion(bf16[2,512,1024]{2,0,1:T(2,128)(2,1)} %all-gather.2.cloned.1.call-done), kind=kLoop, calls=%fused_computation.100 | loop fusion | bytes 4194304 | tf_op jit(solution)/shard_map/slice | solution.py:102
  168.3 40.8 %all-to-all-done.2 = bf16[2,128,1,4096]{1,0,2,3:T(2,128)(2,1)S(1)} async-done(((bf16[2,128,1,4096]{1,0,2,3:T(2,128)(2,1)}), bf16[2,128,1,4096]{1,0,2,3:T(2,128)(2,1)S(1)}, u32[]{:S(2)}, u32[]{:S(2)}) %all-to-all-start.2) | async-done | bytes 2097184 | tf_op jit(solution)/shard_map/all_to_all | solution.py:90
  217.2 29.0 %all_to_all.66 = f32[512,1,512]{2,1,0:T(1,128)S(1)} all-to-all(f32[512,1,512]{2,1,0:T(1,128)S(1)} %copy.138), channel_id=1, replica_groups=mesh['tm'=4,'stn'=8] {'stn'}, dimensions={0} | all-to-all | bytes 2097152 | tf_op jit(solution)/shard_map/all_to_all | solution.py:109
  (63 shorter events, 38.5 us)
Async XLA Ops:
  13.8 6.3 %copy-start.8 = (f32[12,4096]{1,0:T(8,128)S(1)}, f32[12,4096]{1,0:T(8,128)}, u32[]{:S(2)}) copy-start(f32[12,4096]{1,0:T(8,128)} %param.6) | copy-start | bytes 589828
  13.8 30.7 %all-to-all-start = ((bf16[2,128,4096]{2,0,1:T(2,128)(2,1)}), bf16[2,128,4096]{2,0,1:T(2,128)(2,1)S(1)}, u32[]{:S(2)}, u32[]{:S(2)}) async-start(bf16[2,128,4096]{2,0,1:T(2,128)(2,1)} %copy_multiply_fusion), calls=%async_computation | async-start | bytes 4194304 | tf_op jit(solution)/shard_map/all_to_all | solution.py:82
  74.6 3.9 %copy-start = (f32[128,64,64]{0,1,2:T(8,128)S(1)}, f32[128,64,64]{0,1,2:T(8,128)}, u32[]{:S(2)}) copy-start(f32[128,64,64]{0,1,2:T(8,128)} %copy.120) | copy-start | bytes 6291460
  74.6 3.9 %copy-start.3 = (f32[128,64,64]{0,2,1:T(8,128)S(1)}, f32[128,64,64]{0,2,1:T(8,128)}, u32[]{:S(2)}) copy-start(f32[128,64,64]{0,2,1:T(8,128)} %fusion.36) | copy-start | bytes 6291460
  84.0 7.8 %copy-start.1 = (f32[128,64,64]{0,2,1:T(8,128)}, f32[128,64,64]{0,2,1:T(8,128)S(1)}, u32[]{:S(2)}) copy-start(f32[128,64,64]{0,2,1:T(8,128)S(1)} %get-tuple-element.5) | copy-start | bytes 6291460
  99.6 4.6 %copy-start.2 = (f32[128,64,64]{0,2,1:T(8,128)S(1)}, f32[128,64,64]{0,2,1:T(8,128)}, u32[]{:S(2)}) copy-start(f32[128,64,64]{0,2,1:T(8,128)} %copy-done.1) | copy-start | bytes 6291460
  112.4 2.6 %copy-start.5 = (bf16[1,32,4,4096]{3,2,1,0:T(4,128)(2,1)S(1)}, bf16[1,32,4,4096]{3,2,1,0:T(4,128)(2,1)}, u32[]{:S(2)}) copy-start(bf16[1,32,4,4096]{3,2,1,0:T(4,128)(2,1)} %convert_element_type.117) | copy-start | bytes 3145732
  120.3 4.6 %copy-start.9 = (s32[512]{0:T(512)S(1)}, s32[512]{0:T(512)}, u32[]{:S(2)}) copy-start(s32[512]{0:T(512)} %param.8) | copy-start | bytes 6148
  120.3 4.7 %copy-start.7 = (s32[2,64,1024]{2,1,0:T(8,128)S(1)}, s32[2,64,1024]{2,1,0:T(8,128)}, u32[]{:S(2)}) copy-start(s32[2,64,1024]{2,1,0:T(8,128)} %param.7) | copy-start | bytes 1572868
  120.3 29.0 %all-to-all-start.1 = ((bf16[2,32,4,4096]{3,1,0,2:T(8,128)(2,1)}), bf16[2,32,4,4096]{3,1,0,2:T(8,128)(2,1)}, u32[]{:S(2)}, u32[]{:S(2)}) async-start(bf16[2,32,4,4096]{3,1,0,2:T(8,128)(2,1)} %copy.131), calls=%async_computation.1 | async-start | bytes 4194304 | tf_op jit(solution)/shard_map/all_to_all | solution.py:91
  124.9 36.4 %all-gather.2.cloned.1.call-start = ((), (), s32[]{:S(2)}) async-start(), calls=%async_computation.4 | async-start | bytes 2359296 | tf_op jit(solution)/shard_map/all_gather | solution.py:80
  154.9 54.2 %all-to-all-start.2 = ((bf16[2,128,1,4096]{1,0,2,3:T(2,128)(2,1)}), bf16[2,128,1,4096]{1,0,2,3:T(2,128)(2,1)S(1)}, u32[]{:S(2)}, u32[]{:S(2)}) async-start(bf16[2,128,1,4096]{1,0,2,3:T(2,128)(2,1)} %copy.133), calls=%async_computation.2 | async-start | bytes 4194304 | tf_op jit(solution)/shard_map/all_to_all | solution.py:90
  210.6 2.5 copy-start.6
  213.1 1.6 copy-start.4
Sparse Core Ops, SparseCore 0:
  130.4 30.9 all-gather.1
where the time goes:
time: 259 us; the launch traced here: 256 us
  waiting for transfers between devices  85.4 us (33%)
  local copies, waits for them, and re-layouts  64.7 us (25%)
  matrix products  33.2 us (13%)
  blocking collectives  29 us (11%)
  starting transfers between devices  15.6 us (6%)
  other arithmetic  14.1 us (5%)
  between operations  14 us (5%)
    all_to_all x1, waiting for transfers between devices, on_device(): lax.all_to_all(lax.all_to_all(spectra, 'tm', split_axis=2, concat_axis=1,...  40.8 us
    all_to_all x1, blocking collectives, on_device(): lax.all_to_all(channel_power, 'stn', split_axis=0, concat_axis=2, tiled=T...  29 us
    all_to_all x1, waiting for transfers between devices, on_device(): lax.all_to_all(masked, 'tm', split_axis=1, concat_axis=2, tiled=True)  24.3 us
    all_to_all x1, waiting for transfers between devices, on_device(): lax.all_to_all(spectra, 'tm', split_axis=2, concat_axis=1, tiled=True)  19.1 us
    another operation x2, local copies, waits for them, and re-layouts, transform(): imag_cube = imag_in.reshape(batch_rows, RADIX, RADIX)  10.6 us
    convert_element_type x2, local copies, waits for them, and re-layouts, filter_spectra(): chan_real.astype(jnp.bfloat16)  9.09 us
    another operation x2, local copies, waits for them, and re-layouts, transform(): real_cube = real_in.reshape(batch_rows, RADIX, RADIX)  7.84 us
    slice x1, local copies, waits for them, and re-layouts, on_device(): weight_all[1]  6.97 us
  transfers between devices with their start and end apart: 4, of which 4 were waited for; matrix products, arithmetic and copies ran while one was open for 7% of the time, Pallas kernels for 0%

commit v1 on v0

v1 whole, which is shorter than its diff:
```python
import functools
import math

import jax
import jax.numpy as jnp
import numpy as np
from jax import lax
from jax.experimental import pallas as pl
from jax.experimental.pallas import tpu as pltpu
from jax.sharding import PartitionSpec as P

LANES = 128


def fft_list(re, im):
    size = len(re)
    if size == 1:
        return re, im
    even_re, even_im = fft_list(re[0::2], im[0::2])
    odd_re, odd_im = fft_list(re[1::2], im[1::2])
    half = size // 2
    out_re, out_im = [None] * size, [None] * size
    for k in range(half):
        a, b = odd_re[k], odd_im[k]
        if k == 0:
            tr, ti = a, b
        elif 4 * k == size:
            tr, ti = b, -a
        elif 8 * k == size:
            h = math.sqrt(0.5)
            tr, ti = (a + b) * h, (b - a) * h
        elif 8 * k == 3 * size:
            h = math.sqrt(0.5)
            tr, ti = (b - a) * h, (a + b) * (-h)
        else:
            c, s = math.cos(2 * math.pi * k / size), math.sin(2 * math.pi * k / size)
            tr, ti = a * c + b * s, b * c - a * s
        out_re[k], out_re[k + half] = even_re[k] + tr, even_re[k] - tr
        out_im[k], out_im[k + half] = even_im[k] + ti, even_im[k] - ti
    return out_re, out_im


def spectra_kernel(radix, groups, rows, x_ref, taps_ref, twr_ref, twi_ref, th_ref, tl_ref, o_ref, mid_ref, y_ref):
    frames = x_ref.shape[1]
    inputs = x_ref.shape[2]
    taps = taps_ref.shape[0]
    lags = min(taps, frames)
    sub = radix // 4
    per_group = radix // groups
    blocks = inputs // rows

    def unit(step, carry):
        n = step // blocks
        block = step % blocks
        start = block * rows
        if rows % 16 == 0:
            start = pl.multiple_of(start, rows)
        gates = [jnp.where(n >= lag, 1.0, 0.0).astype(jnp.float32) for lag in range(lags)]
        index = [jnp.maximum(n - lag, 0) for lag in range(lags)]
        for a in range(4):
            tile_re, tile_im = [], []
            for j in range(sub):
                c1 = a + 4 * j
                cols = slice(c1 * LANES, (c1 + 1) * LANES)
                acc_re = acc_im = None
                for lag in range(lags):
                    tap = taps_ref[taps - 1 - lag : taps - lag, cols]
                    if lag:
                        tap = tap * gates[lag]
                    pr = x_ref[0, index[lag], pl.ds(start, rows), cols].astype(jnp.float32) * tap
                    pi = x_ref[1, index[lag], pl.ds(start, rows), cols].astype(jnp.float32) * tap
                    acc_re = pr if acc_re is None else acc_re + pr
                    acc_im = pi if acc_im is None else acc_im + pi
                tile_re.append(acc_re)
                tile_im.append(acc_im)
            out_re, out_im = fft_list(tile_re, tile_im)
            for q in range(sub):
                if a * q:
                    c = math.cos(2 * math.pi * a * q / radix)
                    s = math.sin(2 * math.pi * a * q / radix)
                    mid_ref[0, a * sub + q] = out_re[q] * c + out_im[q] * s
                    mid_ref[1, a * sub + q] = out_im[q] * c - out_re[q] * s
                else:
                    mid_ref[0, a * sub + q] = out_re[q]
                    mid_ref[1, a * sub + q] = out_im[q]
        for q in range(sub):
            out_re, out_im = fft_list(
                [mid_ref[0, a * sub + q] for a in range(4)], [mid_ref[1, a * sub + q] for a in range(4)]
            )
            for r in range(4):
                k1 = q + sub * r
                c = twr_ref[k1 : k1 + 1, :]
                s = twi_ref[k1 : k1 + 1, :]
                y_ref[k1 * rows : (k1 + 1) * rows, 0:LANES] = out_re[r] * c + out_im[r] * s
                y_ref[k1 * rows : (k1 + 1) * rows, LANES : 2 * LANES] = out_im[r] * c - out_re[r] * s
        y = y_ref[...]
        high = y.astype(jnp.bfloat16)
        low = (y - high.astype(jnp.float32)).astype(jnp.bfloat16)
        out = (
            jnp.dot(high, th_ref[...], preferred_element_type=jnp.float32)
            + jnp.dot(low, th_ref[...], preferred_element_type=jnp.float32)
            + jnp.dot(high, tl_ref[...], preferred_element_type=jnp.float32)
        ).astype(jnp.bfloat16)
        for k1 in range(radix):
            group, kk = k1 // per_group, k1 % per_group
            for p in range(2):
                o_ref[n * groups + group, p, pl.ds(start, rows), kk * LANES : (kk + 1) * LANES] = out[
                    k1 * rows : (k1 + 1) * rows, p * LANES : (p + 1) * LANES
                ]
        return carry

    lax.fori_loop(0, frames * blocks, unit, 0)


def make_spectra(x, filter_taps, groups):
    _, frames, inputs, channels = x.shape
    radix = channels // LANES
    rows = math.gcd(16, inputs)
    k1 = np.arange(radix)[:, None]
    c2 = np.arange(LANES)
    turn = 2.0 * np.pi * (k1 * c2[None, :]) / channels
    twr, twi = np.cos(turn).astype(np.float32), np.sin(turn).astype(np.float32)
    angle = 2.0 * np.pi * ((c2[:, None] * c2[None, :]) % LANES) / LANES
    cos, sin = np.cos(angle), np.sin(angle)
    table = (np.block([[cos, -sin], [sin, cos]]) / math.sqrt(channels)).astype(np.float32)
    table_high = table.astype(jnp.bfloat16)
    table_low = (table - table_high.astype(np.float32)).astype(jnp.bfloat16)
    return pl.pallas_call(
        functools.partial(spectra_kernel, radix, groups, rows),
        out_shape=jax.ShapeDtypeStruct(
            (frames * groups, 2, inputs, channels // groups), jnp.bfloat16
        ),
        in_specs=[pl.BlockSpec(memory_space=pltpu.VMEM)] * 6,
        out_specs=pl.BlockSpec(memory_space=pltpu.VMEM),
        scratch_shapes=[
            pltpu.VMEM((2, radix, rows, LANES), jnp.float32),
            pltpu.VMEM((radix * rows, 2 * LANES), jnp.float32),
        ],
    )(x, filter_taps, twr, twi, table_high, table_low)


def beam_kernel(scale, x_ref, w_ref, o_ref):
    groups, _, rows, width = x_ref.shape
    x_re = x_ref[:, 0].reshape(groups * rows, width)
    x_im = x_ref[:, 1].reshape(groups * rows, width)

    def block(step, carry):
        size = o_ref.shape[0] // 4
        start = pl.multiple_of(step * size, size)
        w_re = w_ref[0, pl.ds(start, size), :]
        w_im = w_ref[1, pl.ds(start, size), :]
        beam_re = jnp.dot(w_re, x_re, preferred_element_type=jnp.float32) - jnp.dot(
            w_im, x_im, preferred_element_type=jnp.float32
        )
        beam_im = jnp.dot(w_re, x_im, preferred_element_type=jnp.float32) + jnp.dot(
            w_im, x_re, preferred_element_type=jnp.float32
        )
        power = (beam_re * beam_re + beam_im * beam_im) * scale
        o_ref[pl.ds(start, size), :] = power.astype(jnp.bfloat16)
        return carry

    lax.fori_loop(0, 4, block, 0)


def make_power(spectra, weights):
    inputs_all = weights.shape[2]
    if spectra.shape[2] % 16:
        spectra = spectra.transpose(1, 0, 2, 3).reshape(1, 2, inputs_all, spectra.shape[3])
    return pl.pallas_call(
        functools.partial(beam_kernel, 1.0 / inputs_all),
        out_shape=jax.ShapeDtypeStruct((weights.shape[1], spectra.shape[3]), jnp.bfloat16),
        in_specs=[pl.BlockSpec(memory_space=pltpu.VMEM)] * 2,
        out_specs=pl.BlockSpec(memory_space=pltpu.VMEM),
    )(spectra, weights)


def local_weights(beam_weights, station_map, station_flags, tm_size, stn_size):
    inputs_all = beam_weights.shape[2]
    few = inputs_all // (tm_size * stn_size)
    column = jnp.arange(inputs_all, dtype=jnp.int32)
    source, inner = column // few, column % few
    slot_input = (source % stn_size) * (few * tm_size) + (source // stn_size) * few + inner
    flag = station_flags[station_map]
    wanted = (2 * station_map[slot_input // 2] + slot_input % 2).astype(jnp.int32)
    keep = flag[slot_input // 2]
    pick = (jnp.arange(inputs_all, dtype=jnp.int32)[:, None] == wanted[None, :]) & (keep[None, :] != 0)
    low = (beam_weights.astype(jnp.float32) * (1.0 / 32768.0)).astype(jnp.bfloat16)
    return jnp.dot(
        low.reshape(-1, inputs_all), pick.astype(jnp.bfloat16), preferred_element_type=jnp.float32
    ).astype(jnp.bfloat16).reshape(low.shape)


def on_device(tm_size, stn_size, voltages, filter_taps, beam_weights, station_map, station_flags):
    channels = filter_taps.shape[1]
    few = voltages.shape[1] // tm_size
    weights = local_weights(beam_weights, station_map, station_flags, tm_size, stn_size)
    weight_all = lax.all_gather(weights, "stn", axis=1, tiled=True)
    frames = voltages.reshape(2, tm_size, few, channels)
    frames = lax.all_to_all(frames, "tm", split_axis=1, concat_axis=1, tiled=True)
    spectra = make_spectra(frames, filter_taps, stn_size)
    turned = lax.all_to_all(spectra, ("tm", "stn"), split_axis=0, concat_axis=0, tiled=True)
    power = make_power(turned, weight_all)
    beams = power.shape[0] // stn_size
    mine = lax.all_to_all(
        power.reshape(stn_size, beams, -1), "stn", split_axis=0, concat_axis=0, tiled=True
    )
    radix = channels // LANES
    mine = mine.reshape(stn_size, beams, radix // stn_size, LANES).astype(jnp.float32)
    return mine.transpose(1, 3, 0, 2).reshape(beams, 1, channels)


def solution(mesh):
    placed = (P(None, "stn", "tm"), P(), P(None, "stn", None), P(), P())
    body = functools.partial(on_device, mesh.shape["tm"], mesh.shape["stn"])
    return jax.shard_map(
        body, mesh=mesh, in_specs=placed, out_specs=P("stn", "tm", None), check_vma=False
    )
```

time: 259 us -> 159 us (0.61); the launches traced: 256 us -> 159 us
  local copies, waits for them, and re-layouts: 64.7 us -> 27.2 us
  matrix products: 33.2 us -> 1.77 us
  Pallas kernels: 0 us -> 14.6 us
  other arithmetic: 14.1 us -> 0.13 us
  waiting for transfers between devices: 85.4 us -> 72.4 us
  blocking collectives: 29 us -> 18.7 us
  starting transfers between devices: 15.6 us -> 10.4 us
    all_to_all x3 -> x2, waiting for transfers between devices: 84.2 us -> 16.1 us  [the longest x1 8.67 us: on_device(): lax.all_to_all(spectra, ('tm', 'stn'), split_axis=0, concat_axis=0, tiled...]
    all_gather x1, waiting for transfers between devices: 1.22 us -> 56.3 us  [on_device(): weight_all = lax.all_gather(weights, 'stn', axis=1, tiled=True)]
    dot_general x12 -> x1, matrix products: 33.2 us -> 1.77 us  [local_weights(): jnp.dot(low.reshape(-1, inputs_all), pick.astype(jnp.bfloat16), preferred...]
    another operation x5 -> x0, local copies, waits for them, and re-layouts: 20.9 us -> none  [the longest x2 10.6 us: transform(): imag_cube = imag_in.reshape(batch_rows, RADIX, RADIX)]
    convert_element_type x6 -> x0, local copies, waits for them, and re-layouts: 16.3 us -> none  [the longest x2 9.09 us: filter_spectra(): chan_real.astype(jnp.bfloat16)]
    pallas_call x0 -> x2, Pallas kernels: none -> 14.6 us  [the longest x1 8.45 us: make_spectra(): pl.pallas_call(functools.partial(spectra_kernel, radix, groups, rows), ou...]
    gather x3, local copies, waits for them, and re-layouts: 3.46 us -> 17.2 us  [the longest x1 6.86 us: local_weights(): keep = flag[slot_input // 2]]
    all_to_all x1, blocking collectives: 29 us -> 18.7 us  [on_device(): lax.all_to_all(power.reshape(stn_size, beams, -1), 'stn', split_axis=0, c...]
  transfers between devices with their start and end apart: 4 -> 3, of which waited for: 4 -> 3; matrix products, arithmetic and copies ran while one was open for 7% -> 12% of each run, Pallas kernels for 0% -> 0%
where the time goes in v1:
time: 159 us
  waiting for transfers between devices  72.4 us (46%)
  local copies, waits for them, and re-layouts  27.2 us (17%)
  blocking collectives  18.7 us (12%)
  Pallas kernels  14.6 us (9%)
  between operations  13.5 us (8%)
  starting transfers between devices  10.4 us (7%)
  matrix products  1.77 us (1%)
    all_gather x1, waiting for transfers between devices, on_device(): weight_all = lax.all_gather(weights, 'stn', axis=1, tiled=True)  56.3 us
    all_to_all x1, blocking collectives, on_device(): lax.all_to_all(power.reshape(stn_size, beams, -1), 'stn', split_axis=0, c...  18.7 us
    all_to_all x1, waiting for transfers between devices, on_device(): lax.all_to_all(spectra, ('tm', 'stn'), split_axis=0, concat_axis=0, tiled...  8.67 us
    pallas_call x1, Pallas kernels, make_spectra(): pl.pallas_call(functools.partial(spectra_kernel, radix, groups, rows), ou...  8.45 us
    all_to_all x1, waiting for transfers between devices, on_device(): lax.all_to_all(frames, 'tm', split_axis=1, concat_axis=1, tiled=True)  7.42 us
    gather x1, local copies, waits for them, and re-layouts, local_weights(): keep = flag[slot_input // 2]  6.86 us
    gather x1, local copies, waits for them, and re-layouts, local_weights(): station_map[slot_input // 2]  6.86 us
    pallas_call x1, Pallas kernels, make_power(): pl.pallas_call(functools.partial(beam_kernel, 1.0 / inputs_all), out_shap...  6.12 us
  transfers between devices with their start and end apart: 3, of which 3 were waited for; matrix products, arithmetic and copies ran while one was open for 12% of the time, Pallas kernels for 0%

profile of v1, /device:TPU:0, one launch (start us, length us, event | category | flops | bytes accessed | tf_op | source)
XLA Modules:
  0.0 158.7 jit_solution(3705481218985118593)
XLA Ops:
  6.5 0.0 copy-start
  6.5 3.2 %copy.17 = bf16[2,4,32,4096]{3,2,0,1:T(8,128)(2,1)} copy(bf16[2,4,32,4096]{3,2,1,0:T(8,128)(2,1)} %bitcast.11) | data formatting | bytes 4194304 | tf_op jit(solution)/shard_map/reshape | solution.py:198
  9.7 5.3 %all-to-all-start = ((bf16[2,4,32,4096]{3,2,0,1:T(8,128)(2,1)}), bf16[2,4,32,4096]{3,2,0,1:T(8,128)(2,1)S(1)}, u32[]{:S(2)}, u32[]{:S(2)}) async-start(bf16[2,4,32,4096]{3,2,0,1:T(8,128)(2,1)} %copy.17), calls=%async_computation | async-start | bytes 4194304 | tf_op jit(solution)/shard_map/all_to_all | solution.py:199
  15.1 0.0 copy-done.1
  15.1 6.9 %gather_fusion = s32[1024]{0:T(1024)S(1)} fusion(s32[512]{0:T(512)S(1)} %copy-done.1, s32[1024]{0:T(1024)S(1)} %broadcast_clamp_fusion), kind=kCustom, calls=%fused_computation | custom fusion | bytes 12288 | tf_op jit(solution)/shard_map/gather | solution.py:184
  22.0 0.0 copy-done
  22.0 3.5 %gather_fusion.1 = s32[512]{0:T(512)S(1)} fusion(s32[512]{0:T(512)S(1)} %copy-done, s32[1024]{0:T(1024)S(1)} %pad_clamp_fusion), kind=kCustom, calls=%fused_computation.1 | custom fusion | bytes 6144 | tf_op jit(solution)/shard_map/gather | solution.py:183
  25.5 0.0 copy-start.3
  25.5 6.9 %gather_fusion.2 = s32[1024]{0:T(1024)S(1)} fusion(s32[512]{0:T(512)S(1)} %gather_fusion.1, s32[1024]{0:T(1024)S(1)} %broadcast_clamp_fusion), kind=kCustom, calls=%fused_computation.2 | custom fusion | bytes 12288 | tf_op jit(solution)/shard_map/gather | solution.py:185
  32.5 7.4 %all-to-all-done = bf16[2,4,32,4096]{3,2,0,1:T(8,128)(2,1)S(1)} async-done(((bf16[2,4,32,4096]{3,2,0,1:T(8,128)(2,1)}), bf16[2,4,32,4096]{3,2,0,1:T(8,128)(2,1)S(1)}, u32[]{:S(2)}, u32[]{:S(2)}) %all-to-all-start) | async-done | bytes 2097184 | tf_op jit(solution)/shard_map/all_to_all | solution.py:199
  39.9 1.5 copy.18.x_ref
  41.4 8.5 %shard_map.91 = bf16[32,2,32,512]{3,2,1,0:T(8,128)(2,1)} custom-call(bf16[2,4,32,4096]{3,2,1,0:T(8,128)(2,1)} %copy.18.x_ref, f32[12,4096]{1,0:T(8,128)} %taps_ref.1, f32[32,128]{1,0:T(8,128)} %constant.98.clone.twr_ref, f32[32,128]{1,0:T(8,128)} %constant.99.clone.twi_ref, bf16[256,256]{1,0:T(8,128)(2,1)} %constant.100.clone.th_ref, ...), custom_call_target="tpu_custom_call" | custom-call | tf_op jit(solution)/shard_map/pallas_call | solution.py:128
  49.8 5.0 %all-to-all-start.1 = ((bf16[32,2,32,512]{3,2,1,0:T(8,128)(2,1)}), bf16[32,2,32,512]{3,2,1,0:T(8,128)(2,1)S(1)}, u32[]{:S(2)}, u32[]{:S(2)}) async-start(bf16[32,2,32,512]{3,2,1,0:T(8,128)(2,1)} %shard_map.91), calls=%async_computation.1 | async-start | bytes 4194304 | tf_op jit(solution)/shard_map/all_to_all | solution.py:201
  54.8 0.0 all-gather.2.cloned.1.call-start
  54.9 1.8 %fusion.5 = bf16[128,1024]{1,0:T(8,128)(2,1)} fusion(bf16[128,1024]{1,0:T(8,128)(2,1)S(1)} %bitcast.12, s32[1024]{0:T(1024)S(1)} %fusion.20, pred[1024]{0:T(1024)(128)(4,1)S(1)} %broadcast_compare_fusion), kind=kOutput, calls=%fused_computation.8 | convolution fusion | flops 270663680 | bytes 529408 | tf_op jit(solution)/shard_map/dot_general | solution.py:188
  56.7 0.0 all-gather.2.cloned.1.call-update
  56.7 56.3 %all-gather.2.cloned.1.call-done.w_ref = bf16[2,512,1024]{2,1,0:T(8,128)(2,1)} async-done(((bf16[2,64,1024]{2,1,0:T(8,128)(2,1)}), bf16[2,512,1024]{2,1,0:T(8,128)(2,1)}) %all-gather.2.cloned.1.call-update) | async-done | bytes 2097168 | tf_op jit(solution)/shard_map/all_gather | solution.py:197
  113.0 8.7 %all-to-all-done.1.x_ref = bf16[32,2,32,512]{3,2,1,0:T(8,128)(2,1)S(1)} async-done(((bf16[32,2,32,512]{3,2,1,0:T(8,128)(2,1)}), bf16[32,2,32,512]{3,2,1,0:T(8,128)(2,1)S(1)}, u32[]{:S(2)}, u32[]{:S(2)}) %all-to-all-start.1) | async-done | bytes 2097184 | tf_op jit(solution)/shard_map/all_to_all | solution.py:201
  121.7 1.3 copy-done.2
  123.0 6.1 %shard_map.92 = bf16[512,512]{1,0:T(8,128)(2,1)} custom-call(bf16[32,2,32,512]{3,2,1,0:T(8,128)(2,1)} %copy-done.2, bf16[2,512,1024]{2,1,0:T(8,128)(2,1)} %all-gather.2.cloned.1.call-done.w_ref), custom_call_target="tpu_custom_call" | custom-call | tf_op jit(solution)/shard_map/pallas_call | solution.py:169
  129.1 18.7 %all_to_all.15 = bf16[8,64,512]{2,1,0:T(8,128)(2,1)S(1)} all-to-all(bf16[8,64,512]{2,1,0:T(8,128)(2,1)} %bitcast.10), channel_id=1, replica_groups=mesh['tm'=4,'stn'=8] {'stn'}, dimensions={0} | all-to-all | bytes 1048576 | tf_op jit(solution)/shard_map/all_to_all | solution.py:204
  147.8 0.3 reshape.279
  148.2 1.6 %copy.19 = f32[64,128,8,4]{0,3,2,1:T(4,128)S(1)} copy(f32[64,128,8,4]{1,3,0,2:T(4,128)S(1)} %bitcast.9) | data formatting | bytes 2097152 | tf_op jit(solution)/shard_map/reshape | solution.py:209
  149.8 2.1 %copy.20 = f32[64,1,4096]{2,1,0:T(1,128)} copy(f32[64,1,4096]{0,2,1:T(8,128)S(1)} %bitcast.8) | data formatting | bytes 2097152 | tf_op jit(solution)/shard_map/reshape | solution.py:209
  (10 shorter events, 0.1 us)
Async XLA Ops:
  6.5 15.4 %copy-start = (s32[512]{0:T(512)S(1)}, s32[512]{0:T(512)}, u32[]{:S(2)}) copy-start(s32[512]{0:T(512)} %param.13) | copy-start | bytes 6148
  9.7 5.4 %copy-start.1 = (s32[512]{0:T(512)S(1)}, s32[512]{0:T(512)}, u32[]{:S(2)}) copy-start(s32[512]{0:T(512)} %param.12) | copy-start | bytes 6148
  9.7 30.2 %all-to-all-start = ((bf16[2,4,32,4096]{3,2,0,1:T(8,128)(2,1)}), bf16[2,4,32,4096]{3,2,0,1:T(8,128)(2,1)S(1)}, u32[]{:S(2)}, u32[]{:S(2)}) async-start(bf16[2,4,32,4096]{3,2,0,1:T(8,128)(2,1)} %copy.17), calls=%async_computation | async-start | bytes 4194304 | tf_op jit(solution)/shard_map/all_to_all | solution.py:199
  25.5 6.9 %copy-start.3 = (s32[2,64,1024]{2,1,0:T(8,128)S(1)}, s32[2,64,1024]{2,1,0:T(8,128)}, u32[]{:S(2)}) copy-start(s32[2,64,1024]{2,1,0:T(8,128)} %param.11) | copy-start | bytes 1572868
  49.8 71.9 %all-to-all-start.1 = ((bf16[32,2,32,512]{3,2,1,0:T(8,128)(2,1)}), bf16[32,2,32,512]{3,2,1,0:T(8,128)(2,1)S(1)}, u32[]{:S(2)}, u32[]{:S(2)}) async-start(bf16[32,2,32,512]{3,2,1,0:T(8,128)(2,1)} %shard_map.91), calls=%async_computation.1 | async-start | bytes 4194304 | tf_op jit(solution)/shard_map/all_to_all | solution.py:201
  54.8 58.2 %all-gather.2.cloned.1.call-start = ((), (), s32[]{:S(2)}) async-start(), calls=%async_computation.3 | async-start | bytes 2359296 | tf_op jit(solution)/shard_map/all_gather | solution.py:197
  121.7 1.3 copy-start.2
Sparse Core Ops, SparseCore 0:
  57.3 55.7 all-gather.1

commit v2 on v1

v2 whole, which is shorter than its diff:
```python
import functools
import math

import jax
import jax.numpy as jnp
import numpy as np
from jax import lax
from jax.experimental import pallas as pl
from jax.experimental.pallas import tpu as pltpu
from jax.sharding import PartitionSpec as P

LANES = 128


def fft_list(re, im):
    size = len(re)
    if size == 1:
        return re, im
    even_re, even_im = fft_list(re[0::2], im[0::2])
    odd_re, odd_im = fft_list(re[1::2], im[1::2])
    half = size // 2
    out_re, out_im = [None] * size, [None] * size
    for k in range(half):
        a, b = odd_re[k], odd_im[k]
        if k == 0:
            tr, ti = a, b
        elif 4 * k == size:
            tr, ti = b, -a
        elif 8 * k == size:
            h = math.sqrt(0.5)
            tr, ti = (a + b) * h, (b - a) * h
        elif 8 * k == 3 * size:
            h = math.sqrt(0.5)
            tr, ti = (b - a) * h, (a + b) * (-h)
        else:
            c, s = math.cos(2 * math.pi * k / size), math.sin(2 * math.pi * k / size)
            tr, ti = a * c + b * s, b * c - a * s
        out_re[k], out_re[k + half] = even_re[k] + tr, even_re[k] - tr
        out_im[k], out_im[k + half] = even_im[k] + ti, even_im[k] - ti
    return out_re, out_im


def transform_unit(radix, rows, frames, n, load, store, taps_ref, twr_ref, twi_ref, th_ref, tl_ref, mid_ref, y_ref):
    taps = taps_ref.shape[0]
    lags = min(taps, frames)
    sub = radix // 4
    gates = [jnp.where(n >= lag, 1.0, 0.0).astype(jnp.float32) for lag in range(lags)]
    index = [jnp.maximum(n - lag, 0) for lag in range(lags)]
    for a in range(4):
        tile_re, tile_im = [], []
        for j in range(sub):
            c1 = a + 4 * j
            cols = slice(c1 * LANES, (c1 + 1) * LANES)
            acc_re = acc_im = None
            for lag in range(lags):
                tap = taps_ref[taps - 1 - lag : taps - lag, cols]
                if lag:
                    tap = tap * gates[lag]
                pr = load(0, index[lag], cols).astype(jnp.float32) * tap
                pi = load(1, index[lag], cols).astype(jnp.float32) * tap
                acc_re = pr if acc_re is None else acc_re + pr
                acc_im = pi if acc_im is None else acc_im + pi
            tile_re.append(acc_re)
            tile_im.append(acc_im)
        out_re, out_im = fft_list(tile_re, tile_im)
        for q in range(sub):
            if a * q:
                c = math.cos(2 * math.pi * a * q / radix)
                s = math.sin(2 * math.pi * a * q / radix)
                mid_ref[0, a * sub + q] = out_re[q] * c + out_im[q] * s
                mid_ref[1, a * sub + q] = out_im[q] * c - out_re[q] * s
            else:
                mid_ref[0, a * sub + q] = out_re[q]
                mid_ref[1, a * sub + q] = out_im[q]
    for q in range(sub):
        out_re, out_im = fft_list(
            [mid_ref[0, a * sub + q] for a in range(4)], [mid_ref[1, a * sub + q] for a in range(4)]
        )
        for r in range(4):
            k1 = q + sub * r
            c = twr_ref[k1 : k1 + 1, :]
            s = twi_ref[k1 : k1 + 1, :]
            y_ref[k1 * rows : (k1 + 1) * rows, 0:LANES] = out_re[r] * c + out_im[r] * s
            y_ref[k1 * rows : (k1 + 1) * rows, LANES : 2 * LANES] = out_im[r] * c - out_re[r] * s
    y = y_ref[...]
    high = y.astype(jnp.bfloat16)
    low = (y - high.astype(jnp.float32)).astype(jnp.bfloat16)
    out = (
        jnp.dot(high, th_ref[...], preferred_element_type=jnp.float32)
        + jnp.dot(low, th_ref[...], preferred_element_type=jnp.float32)
        + jnp.dot(high, tl_ref[...], preferred_element_type=jnp.float32)
    ).astype(jnp.bfloat16)
    for k1 in range(radix):
        for p in range(2):
            store(k1, p, out[k1 * rows : (k1 + 1) * rows, p * LANES : (p + 1) * LANES])


def spectra_kernel(radix, groups, rows, x_ref, taps_ref, twr_ref, twi_ref, th_ref, tl_ref, o_ref, mid_ref, y_ref):
    frames = x_ref.shape[1]
    blocks = x_ref.shape[2] // rows
    per_group = radix // groups

    def unit(step, carry):
        n = step // blocks
        start = step % blocks * rows
        if rows % 16 == 0:
            start = pl.multiple_of(start, rows)

        def load(p, frame, cols):
            return x_ref[p, frame, pl.ds(start, rows), cols]

        def store(k1, p, value):
            kk = k1 % per_group
            o_ref[n * groups + k1 // per_group, p, pl.ds(start, rows), kk * LANES : (kk + 1) * LANES] = value

        transform_unit(
            radix, rows, frames, n, load, store, taps_ref, twr_ref, twi_ref, th_ref, tl_ref, mid_ref, y_ref
        )
        return carry

    lax.fori_loop(0, frames * blocks, unit, 0)


def tables(channels):
    radix = channels // LANES
    k1 = np.arange(radix)[:, None]
    c2 = np.arange(LANES)
    turn = 2.0 * np.pi * (k1 * c2[None, :]) / channels
    twr, twi = np.cos(turn).astype(np.float32), np.sin(turn).astype(np.float32)
    angle = 2.0 * np.pi * ((c2[:, None] * c2[None, :]) % LANES) / LANES
    cos, sin = np.cos(angle), np.sin(angle)
    table = (np.block([[cos, -sin], [sin, cos]]) / math.sqrt(channels)).astype(np.float32)
    table_high = table.astype(jnp.bfloat16)
    table_low = (table - table_high.astype(np.float32)).astype(jnp.bfloat16)
    return twr, twi, table_high, table_low


def make_spectra(x, filter_taps, groups):
    _, frames, inputs, channels = x.shape
    radix = channels // LANES
    rows = math.gcd(16, inputs)
    return pl.pallas_call(
        functools.partial(spectra_kernel, radix, groups, rows),
        out_shape=jax.ShapeDtypeStruct(
            (frames * groups, 2, inputs, channels // groups), jnp.bfloat16
        ),
        in_specs=[pl.BlockSpec(memory_space=pltpu.VMEM)] * 6,
        out_specs=pl.BlockSpec(memory_space=pltpu.VMEM),
        scratch_shapes=[
            pltpu.VMEM((2, radix, rows, LANES), jnp.float32),
            pltpu.VMEM((radix * rows, 2 * LANES), jnp.float32),
        ],
    )(x, filter_taps, *tables(channels))


def beam_kernel(scale, x_ref, w_ref, o_ref):
    groups, _, rows, width = x_ref.shape
    x_re = x_ref[:, 0].reshape(groups * rows, width)
    x_im = x_ref[:, 1].reshape(groups * rows, width)

    def block(step, carry):
        size = o_ref.shape[0] // 4
        start = pl.multiple_of(step * size, size)
        w_re = w_ref[0, pl.ds(start, size), :]
        w_im = w_ref[1, pl.ds(start, size), :]
        beam_re = jnp.dot(w_re, x_re, preferred_element_type=jnp.float32) - jnp.dot(
            w_im, x_im, preferred_element_type=jnp.float32
        )
        beam_im = jnp.dot(w_re, x_im, preferred_element_type=jnp.float32) + jnp.dot(
            w_im, x_re, preferred_element_type=jnp.float32
        )
        power = (beam_re * beam_re + beam_im * beam_im) * scale
        o_ref[pl.ds(start, size), :] = power.astype(jnp.bfloat16)
        return carry

    lax.fori_loop(0, 4, block, 0)


def make_power(spectra, weights):
    inputs_all = weights.shape[2]
    if spectra.shape[2] % 16:
        spectra = spectra.transpose(1, 0, 2, 3).reshape(1, 2, inputs_all, spectra.shape[3])
    return pl.pallas_call(
        functools.partial(beam_kernel, 1.0 / inputs_all),
        out_shape=jax.ShapeDtypeStruct((weights.shape[1], spectra.shape[3]), jnp.bfloat16),
        in_specs=[pl.BlockSpec(memory_space=pltpu.VMEM)] * 2,
        out_specs=pl.BlockSpec(memory_space=pltpu.VMEM),
    )(spectra, weights)


def local_weights(beam_weights, station_map, station_flags, tm_size, stn_size):
    inputs_all = beam_weights.shape[2]
    few = inputs_all // (tm_size * stn_size)
    column = jnp.arange(inputs_all, dtype=jnp.int32)
    source, inner = column // few, column % few
    slot_input = (source % stn_size) * (few * tm_size) + (source // stn_size) * few + inner
    flag = station_flags[station_map]
    wanted = (2 * station_map[slot_input // 2] + slot_input % 2).astype(jnp.int32)
    keep = flag[slot_input // 2]
    pick = (jnp.arange(inputs_all, dtype=jnp.int32)[:, None] == wanted[None, :]) & (keep[None, :] != 0)
    low = (beam_weights.astype(jnp.float32) * (1.0 / 32768.0)).astype(jnp.bfloat16)
    return jnp.dot(
        low.reshape(-1, inputs_all), pick.astype(jnp.bfloat16), preferred_element_type=jnp.float32
    ).astype(jnp.bfloat16).reshape(low.shape)


def fused_kernel(
    tm, stn, radix, scale,
    v_ref, w_ref, wanted_ref, flag_ref, taps_ref, twr_ref, twi_ref, th_ref, tl_ref,
    o_ref,
    xbuf, sbuf, rbuf, wbuf, acc, pbuf, qbuf, mid_ref, y_ref,
    v_send, v_recv, up_send, up_recv, down_send, down_recv, side_send, side_recv,
    s_send, s_recv, p_send, p_recv, o_sem,
):
    halves, rows = xbuf.shape[0], xbuf.shape[3]
    chips = stn // 2
    per_group = radix // stn
    me_t, me_s = lax.axis_index("tm"), lax.axis_index("stn")
    z, core = me_s // 2, me_s % 2
    me = me_t * stn + me_s
    width = rbuf.shape[4]

    def remote(src, dst, send, recv, t, s):
        return pltpu.make_async_remote_copy(
            src_ref=src, dst_ref=dst, send_sem=send, recv_sem=recv,
            device_id=(t, s), device_id_type=pl.DeviceIdType.MESH,
        )

    def settle(ref, sem):
        pltpu.make_async_copy(ref, ref, sem).wait()

    barrier = pltpu.get_barrier_semaphore()

    def greet(d, carry):
        other = lax.rem(me + d, tm * stn)
        pl.semaphore_signal(
            barrier, inc=1, device_id=(other // stn, other % stn), device_id_type=pl.DeviceIdType.MESH
        )
        return carry

    lax.fori_loop(1, tm * stn, greet, 0)
    pl.semaphore_wait(barrier, tm * stn - 1)

    for h in range(halves):
        for d in range(1, tm):
            t = lax.rem(me_t + d, tm)
            remote(
                v_ref.at[:, t, h * rows : (h + 1) * rows], xbuf.at[h, :, me_t],
                v_send.at[h], v_recv.at[h], t, me_s,
            ).start()
        pltpu.make_async_copy(
            v_ref.at[:, me_t, h * rows : (h + 1) * rows], xbuf.at[h, :, me_t], v_recv.at[h]
        ).start()

    beams, inputs_all = w_ref.shape[1], w_ref.shape[2]
    low = (w_ref[...].astype(jnp.float32) * (flag_ref[...] * (1.0 / 32768.0))[None]).astype(jnp.bfloat16)
    low = low.reshape(2 * beams, inputs_all)
    step = min(256, inputs_all)
    for first in range(0, inputs_all, step):
        station = lax.broadcasted_iota(jnp.int32, (inputs_all, step), 0)
        pick = jnp.where(station == wanted_ref[:, first : first + step], 1.0, 0.0).astype(jnp.bfloat16)
        wbuf[me_s, :, first : first + step] = jnp.dot(
            low, pick, preferred_element_type=jnp.float32
        ).astype(jnp.bfloat16)

    def to_side(block):
        slot = 2 * block + core
        remote(wbuf.at[slot], wbuf.at[slot], side_send.at[block], side_recv.at[block], me_t, 2 * z + 1 - core).start()

    def chain_send(r):
        @pl.when((z >= r) & (z < chips - 1))
        def _():
            slot = 2 * (z - r) + core
            remote(wbuf.at[slot], wbuf.at[slot], up_send.at[r], up_recv.at[r], me_t, me_s + 2).start()

        @pl.when((z + r <= chips - 1) & (z > 0))
        def _():
            slot = 2 * (z + r) + core
            remote(wbuf.at[slot], wbuf.at[slot], down_send.at[r], down_recv.at[r], me_t, me_s - 2).start()

    def chain_recv(r):
        @pl.when(z - 1 - r >= 0)
        def _():
            settle(wbuf.at[0], up_recv.at[r])
            to_side(z - 1 - r)

        @pl.when(z + 1 + r <= chips - 1)
        def _():
            settle(wbuf.at[0], down_recv.at[r])
            to_side(z + 1 + r)

    to_side(z)
    chain_send(0)
    for r in range(1, chips - 1):
        if r < chips - 2:
            chain_recv(r - 1)
            chain_send(r)

    for h in range(halves):
        settle(xbuf.at[h], v_recv.at[h])

        def frame(j, carry):
            n = lax.rem(me_t + j, tm)

            def load(p, index, cols):
                return xbuf[h, p, index, :, cols]

            def store(k1, p, value):
                kk = k1 % per_group
                sbuf[h, n * stn + k1 // per_group, p, :, kk * LANES : (kk + 1) * LANES] = value

            transform_unit(
                radix, rows, tm, n, load, store, taps_ref, twr_ref, twi_ref, th_ref, tl_ref, mid_ref, y_ref
            )

            def send(e, inner):
                s = lax.rem(me_s + e, stn)
                remote(
                    sbuf.at[h, n * stn + s], rbuf.at[h, me], s_send.at[h], s_recv.at[h], n, s
                ).start()
                return inner

            lax.fori_loop(1, stn, send, 0)

            @pl.when(j > 0)
            def _():
                send(0, 0)

            @pl.when(j == 0)
            def _():
                pltpu.make_async_copy(sbuf.at[h, me], rbuf.at[h, me], s_recv.at[h]).start()

            return carry

        lax.fori_loop(0, tm, frame, 0)
        if h == 0:
            if chips > 2:
                chain_recv(chips - 3)
                chain_send(chips - 2)
    if chips > 1:
        chain_recv(chips - 2)

    for block in range(chips):
        settle(wbuf.at[0], side_recv.at[block])

    def beams_of(h, pair):
        cols = slice(h * inputs_all // halves, (h + 1) * inputs_all // halves)
        w = wbuf[pl.ds(2 * pair, 2), :, cols].reshape(4 * beams, inputs_all // halves)
        x_re = rbuf[h, :, 0].reshape(inputs_all // halves, width)
        x_im = rbuf[h, :, 1].reshape(inputs_all // halves, width)
        by_re = jnp.dot(w, x_re, preferred_element_type=jnp.float32).reshape(2, 2, beams, width)
        by_im = jnp.dot(w, x_im, preferred_element_type=jnp.float32).reshape(2, 2, beams, width)
        return by_re[:, 0] - by_im[:, 1], by_im[:, 0] + by_re[:, 1]

    for h in range(halves - 1):
        settle(rbuf.at[h], s_recv.at[h])

        def collect(pair, carry):
            beam_re, beam_im = beams_of(h, pair)
            two = pl.ds(2 * pair, 2)
            if h:
                beam_re, beam_im = beam_re + acc[0, two], beam_im + acc[1, two]
            acc[0, two] = beam_re
            acc[1, two] = beam_im
            return carry

        lax.fori_loop(0, chips, collect, 0)

    settle(rbuf.at[halves - 1], s_recv.at[halves - 1])

    def finish(i, carry):
        pair = lax.rem(z + 1 + i, chips)
        beam_re, beam_im = beams_of(halves - 1, pair)
        two = pl.ds(2 * pair, 2)
        if halves > 1:
            beam_re, beam_im = beam_re + acc[0, two], beam_im + acc[1, two]
        qbuf[two] = ((beam_re * beam_re + beam_im * beam_im) * scale).astype(jnp.bfloat16)
        other = 2 * pair + 1 - core
        same = 2 * pair + core
        remote(qbuf.at[other], pbuf.at[me_s], p_send, p_recv, me_t, other).start()

        @pl.when(i < chips - 1)
        def _():
            remote(qbuf.at[same], pbuf.at[me_s], p_send, p_recv, me_t, same).start()

        @pl.when(i == chips - 1)
        def _():
            pltpu.make_async_copy(qbuf.at[me_s], pbuf.at[me_s], p_recv).start()

        return carry

    lax.fori_loop(0, chips, finish, 0)

    for h in range(halves):
        settle(xbuf.at[h, :, 0 : tm - 1], v_send.at[h])
        settle(sbuf.at[h, 0 : tm * stn - 1], s_send.at[h])
    for block in range(chips):
        settle(wbuf.at[0], side_send.at[block])
    for r in range(chips - 1):
        @pl.when((z >= r) & (z < chips - 1))
        def _():
            settle(wbuf.at[0], up_send.at[r])

        @pl.when((z + r <= chips - 1) & (z > 0))
        def _():
            settle(wbuf.at[0], down_send.at[r])
    settle(qbuf.at[0 : stn - 1], p_send)
    settle(pbuf, p_recv)
    out = pltpu.make_async_copy(pbuf, o_ref, o_sem)
    out.start()
    out.wait()


def fused(tm, stn, voltages, filter_taps, beam_weights, station_map, station_flags):
    channels = filter_taps.shape[1]
    radix = channels // LANES
    few = voltages.shape[1] // tm
    halves = 2
    rows = few // halves
    width = channels // stn
    beams, inputs_all = beam_weights.shape[1], beam_weights.shape[2]
    chips = stn // 2
    wanted = (2 * station_map[:, None] + jnp.arange(2, dtype=jnp.int32)[None, :]).reshape(
        stn, tm, halves, rows
    ).transpose(2, 1, 0, 3).reshape(1, inputs_all)
    flags = jnp.repeat(station_flags, 2).astype(jnp.float32).reshape(1, inputs_all)
    dma = pltpu.SemaphoreType.DMA
    vmem = pl.BlockSpec(memory_space=pltpu.VMEM)
    hbm = pl.BlockSpec(memory_space=pl.ANY)
    low = jnp.bfloat16
    return pl.pallas_call(
        functools.partial(fused_kernel, tm, stn, radix, 1.0 / inputs_all),
        out_shape=jax.ShapeDtypeStruct((stn, beams, width), low),
        in_specs=[hbm] + [vmem] * 8,
        out_specs=hbm,
        scratch_shapes=[
            pltpu.VMEM((halves, 2, tm, rows, channels), low),
            pltpu.VMEM((halves, tm * stn, 2, rows, width), low),
            pltpu.VMEM((halves, tm * stn, 2, rows, width), low),
            pltpu.VMEM((stn, 2 * beams, inputs_all), low),
            pltpu.VMEM((2, stn, beams, width), jnp.float32),
            pltpu.VMEM((stn, beams, width), low),
            pltpu.VMEM((stn, beams, width), low),
            pltpu.VMEM((2, radix, rows, LANES), jnp.float32),
            pltpu.VMEM((radix * rows, 2 * LANES), jnp.float32),
            dma((halves,)), dma((halves,)),
            dma((chips,)), dma((chips,)), dma((chips,)), dma((chips,)), dma((chips,)), dma((chips,)),
            dma((halves,)), dma((halves,)), dma, dma, dma,
        ],
        compiler_params=pltpu.CompilerParams(collective_id=0, has_side_effects=True),
    )(
        voltages.reshape(2, tm, few, channels), beam_weights, wanted, flags, filter_taps, *tables(channels)
    )


def on_device(tm_size, stn_size, voltages, filter_taps, beam_weights, station_map, station_flags):
    channels = filter_taps.shape[1]
    few = voltages.shape[1] // tm_size
    if few % 32 == 0 and stn_size % 2 == 0:
        mine = fused(tm_size, stn_size, voltages, filter_taps, beam_weights, station_map, station_flags)
        beams = mine.shape[1]
    else:
        weights = local_weights(beam_weights, station_map, station_flags, tm_size, stn_size)
        weight_all = lax.all_gather(weights, "stn", axis=1, tiled=True)
        frames = voltages.reshape(2, tm_size, few, channels)
        frames = lax.all_to_all(frames, "tm", split_axis=1, concat_axis=1, tiled=True)
        spectra = make_spectra(frames, filter_taps, stn_size)
        turned = lax.all_to_all(spectra, ("tm", "stn"), split_axis=0, concat_axis=0, tiled=True)
        power = make_power(turned, weight_all)
        beams = power.shape[0] // stn_size
        mine = lax.all_to_all(
            power.reshape(stn_size, beams, -1), "stn", split_axis=0, concat_axis=0, tiled=True
        )
    radix = channels // LANES
    mine = mine.reshape(stn_size, beams, radix // stn_size, LANES).astype(jnp.float32)
    return mine.transpose(1, 3, 0, 2).reshape(beams, 1, channels)


def solution(mesh):
    placed = (P(None, "stn", "tm"), P(), P(None, "stn", None), P(), P())
    body = functools.partial(on_device, mesh.shape["tm"], mesh.shape["stn"])
    return jax.shard_map(
        body, mesh=mesh, in_specs=placed, out_specs=P("stn", "tm", None), check_vma=False
    )
```

time: 159 us -> 90.2 us (0.57)
  waiting for transfers between devices: 72.4 us -> 0 us
  Pallas kernels: 14.6 us -> 81.4 us
  local copies, waits for them, and re-layouts: 27.2 us -> 7.03 us
  blocking collectives: 18.7 us -> 0 us
  between operations: 13.5 us -> 0.05 us
  starting transfers between devices: 10.4 us -> 0 us
  matrix products: 1.77 us -> 0 us
    pallas_call x2 -> x1, Pallas kernels: 14.6 us -> 81.4 us  [fused(): pl.pallas_call(functools.partial(fused_kernel, tm, stn, radix, 1.0 / inpu...]
    all_gather x1 -> x0, waiting for transfers between devices: 56.3 us -> none  [on_device(): weight_all = lax.all_gather(weights, 'stn', axis=1, tiled=True)]
    all_to_all x1 -> x0, blocking collectives: 18.7 us -> none  [on_device(): lax.all_to_all(power.reshape(stn_size, beams, -1), 'stn', split_axis=0, c...]
    gather x3 -> x0, local copies, waits for them, and re-layouts: 17.2 us -> none  [the longest x1 6.86 us: local_weights(): keep = flag[slot_input // 2]]
    all_to_all x2 -> x0, waiting for transfers between devices: 16.1 us -> none  [the longest x1 8.67 us: on_device(): lax.all_to_all(spectra, ('tm', 'stn'), split_axis=0, concat_axis=0, tiled...]
    all_to_all x2 -> x0, starting transfers between devices: 10.3 us -> none  [the longest x1 5.32 us: on_device(): lax.all_to_all(frames, 'tm', split_axis=1, concat_axis=1, tiled=True)]
    reshape x1, local copies, waits for them, and re-layouts: 3.16 us -> 0.69 us  [fused(): wanted = (2 * station_map[:, None] + jnp.arange(2, dtype=jnp.int32)[None,...]
    dot_general x1 -> x0, matrix products: 1.77 us -> none  [local_weights(): jnp.dot(low.reshape(-1, inputs_all), pick.astype(jnp.bfloat16), preferred...]
  transfers between devices with their start and end apart: 3 -> 0, of which waited for: 3 -> 0; matrix products, arithmetic and copies ran while one was open for 12% -> 0% of each run, Pallas kernels for 0% -> 0%
where the time goes in v2:
time: 90.2 us; the launch traced here: 89.9 us
  Pallas kernels  81.4 us (90%)
  local copies, waits for them, and re-layouts  7.03 us (8%)
  other arithmetic  1.44 us (2%)
    pallas_call x1, Pallas kernels, fused(): pl.pallas_call(functools.partial(fused_kernel, tm, stn, radix, 1.0 / inpu...  81.4 us
    reshape x3, local copies, waits for them, and re-layouts, on_device(): return mine.transpose(1, 3, 0, 2).reshape(beams, 1, channels)  5.06 us

profile of v2, /device:TPU:0, one launch (start us, length us, event | category | flops | bytes accessed | tf_op | source)
XLA Modules:
  0.0 89.9 jit_solution(3402385242015604809)
XLA Ops:
  0.0 0.7 broadcast_multiply_fusion
  0.7 0.7 convert_element_type.18
  1.4 0.1 add.26
  1.5 0.1 add.22
  1.6 0.1 copy.11
  1.7 0.1 add_bitcast_fusion
  1.8 0.1 copy.12
  1.8 0.7 reshape.36.wanted_ref
  2.5 0.1 broadcast_in_dim.2
  2.7 0.8 convert_element_type.19.flag_ref
  3.4 81.4 %shard_map.91 = bf16[8,64,512]{2,1,0:T(8,128)(2,1)} custom-call(bf16[2,4,32,4096]{3,2,1,0:T(8,128)(2,1)} %bitcast.10, s32[2,64,1024]{2,1,0:T(8,128)} %w_ref.1, s32[1,1024]{1,0:T(1,128)} %reshape.36.wanted_ref, f32[1,1024]{1,0:T(1,128)} %convert_element_type.19.flag_ref, f32[12,4096]{1,0:T(8,128)} %taps_ref.1, f32[32,128]{1,0:T(8,128)} %constant.10.clone.twr_ref, ...), custom_call_target="tpu_custom_call" | custom-call | tf_op jit(solution)/shard_map/pallas_call | solution.py:431
  84.8 1.4 %reshape.43 = f32[8,64,4,128]{3,2,1,0:T(4,128)S(1)} reshape(bf16[8,64,512]{2,1,0:T(8,128)(2,1)} %shard_map.91) | data formatting | bytes 1572864 | tf_op jit(solution)/shard_map/reshape | solution.py:476
  86.2 1.6 %copy.13 = f32[8,64,4,128]{1,2,0,3:T(4,128)S(1)} copy(f32[8,64,4,128]{3,2,1,0:T(4,128)S(1)} %reshape.43) | data formatting | bytes 2097152 | tf_op jit(solution)/shard_map/reshape | solution.py:476
  87.8 2.1 %copy.14 = f32[64,1,4096]{2,1,0:T(1,128)} copy(f32[64,1,4096]{0,2,1:T(8,128)S(1)} %bitcast.9) | data formatting | bytes 2097152 | tf_op jit(solution)/shard_map/reshape | solution.py:476
  (2 shorter events, 0.0 us)

commit v3 on v2

--- a/solution.py
+++ b/solution.py
@@ -206,7 +206,7 @@
 
 def fused_kernel(
     tm, stn, radix, scale,
-    v_ref, w_ref, wanted_ref, flag_ref, taps_ref, twr_ref, twi_ref, th_ref, tl_ref,
+    v_ref, w_ref, map_ref, flag_ref, taps_ref, twr_ref, twi_ref, th_ref, tl_ref,
     o_ref,
     xbuf, sbuf, rbuf, wbuf, acc, pbuf, qbuf, mid_ref, y_ref,
     v_send, v_recv, up_send, up_recv, down_send, down_recv, side_send, side_recv,
@@ -239,7 +239,71 @@
         return carry
 
     lax.fori_loop(1, tm * stn, greet, 0)
+    beams, inputs_all = w_ref.shape[1], w_ref.shape[2]
+    stations = map_ref.shape[1]
+    few = halves * rows
+    number = jnp.broadcast_to(map_ref[...], (8, stations))
+    flags = jnp.broadcast_to(flag_ref[...], (8, stations))
+    row = lax.broadcasted_iota(jnp.int32, (8, stations), 0)
+    facts = jnp.where(row == 0, number >> 4, jnp.where(row == 1, number & 15, flags))
+    facts = facts.astype(jnp.float32).astype(jnp.bfloat16)
+    step = min(256, inputs_all)
+
+    def look_up(slot):
+        slots = lax.broadcasted_iota(jnp.int32, (stations, step), 0)
+        pick = jnp.where(slots == slot, 1.0, 0.0).astype(jnp.bfloat16)
+        return jnp.dot(facts, pick, preferred_element_type=jnp.float32)
+
+    low = []
+    for first in range(0, inputs_all, step):
+        column = first + lax.broadcasted_iota(jnp.int32, (1, step), 1)
+        keep = look_up(column >> 1)[2:3] * (1.0 / 32768.0)
+        low.append((w_ref[:, :, first : first + step].astype(jnp.float32) * keep[None]).astype(jnp.bfloat16))
+    low = jnp.concatenate(low, axis=2).reshape(2 * beams, inputs_all)
+    for first in range(0, inputs_all, step):
+        column = first + lax.broadcasted_iota(jnp.int32, (1, step), 1)
+        part = inputs_all // halves
+        h, rest = lax.div(column, part), lax.rem(column, part)
+        source, inner = lax.div(rest, rows), lax.rem(rest, rows)
+        ours = lax.rem(source, stn) * (few * tm) + lax.div(source, stn) * few + h * rows + inner
+        found = look_up(ours >> 1)
+        wanted = (found[0:1] * 32.0 + found[1:2] * 2.0).astype(jnp.int32) + (ours & 1)
+        station = lax.broadcasted_iota(jnp.int32, (inputs_all, step), 0)
+        pick = jnp.where(station == wanted, 1.0, 0.0).astype(jnp.bfloat16)
+        wbuf[me_s, :, first : first + step] = jnp.dot(
+            low, pick, preferred_element_type=jnp.float32
+        ).astype(jnp.bfloat16)
+
     pl.semaphore_wait(barrier, tm * stn - 1)
+
+    def to_side(block):
+        slot = 2 * block + core
+        remote(wbuf.at[slot], wbuf.at[slot], side_send.at[block], side_recv.at[block], me_t, 2 * z + 1 - core).start()
+
+    def chain_send(r):
+        @pl.when((z >= r) & (z < chips - 1))
+        def _():
+            slot = 2 * (z - r) + core
+            remote(wbuf.at[slot], wbuf.at[slot], up_send.at[r], up_recv.at[r], me_t, me_s + 2).start()
+
+        @pl.when((z + r <= chips - 1) & (z > 0))
+        def _():
+            slot = 2 * (z + r) + core
+            remote(wbuf.at[slot], wbuf.at[slot], down_send.at[r], down_recv.at[r], me_t, me_s - 2).start()
+
+    def chain_recv(r):
+        @pl.when(z - 1 - r >= 0)
+        def _():
+            settle(wbuf.at[0], up_recv.at[r])
+            to_side(z - 1 - r)
+
+        @pl.when(z + 1 + r <= chips - 1)
+        def _():
+            settle(wbuf.at[0], down_recv.at[r])
+            to_side(z + 1 + r)
+
+    chain_send(0)
+    to_side(z)
 
     for h in range(halves):
         for d in range(1, tm):
@@ -252,45 +316,6 @@
             v_ref.at[:, me_t, h * rows : (h + 1) * rows], xbuf.at[h, :, me_t], v_recv.at[h]
         ).start()
 
-    beams, inputs_all = w_ref.shape[1], w_ref.shape[2]
-    low = (w_ref[...].astype(jnp.float32) * (flag_ref[...] * (1.0 / 32768.0))[None]).astype(jnp.bfloat16)
-    low = low.reshape(2 * beams, inputs_all)
-    step = min(256, inputs_all)
-    for first in range(0, inputs_all, step):
-        station = lax.broadcasted_iota(jnp.int32, (inputs_all, step), 0)
-        pick = jnp.where(station == wanted_ref[:, first : first + step], 1.0, 0.0).astype(jnp.bfloat16)
-        wbuf[me_s, :, first : first + step] = jnp.dot(
-            low, pick, preferred_element_type=jnp.float32
-        ).astype(jnp.bfloat16)
-
-    def to_side(block):
-        slot = 2 * block + core
-        remote(wbuf.at[slot], wbuf.at[slot], side_send.at[block], side_recv.at[block], me_t, 2 * z + 1 - core).start()
-
-    def chain_send(r):
-        @pl.when((z >= r) & (z < chips - 1))
-        def _():
-            slot = 2 * (z - r) + core
-            remote(wbuf.at[slot], wbuf.at[slot], up_send.at[r], up_recv.at[r], me_t, me_s + 2).start()
-
-        @pl.when((z + r <= chips - 1) & (z > 0))
-        def _():
-            slot = 2 * (z + r) + core
-            remote(wbuf.at[slot], wbuf.at[slot], down_send.at[r], down_recv.at[r], me_t, me_s - 2).start()
-
-    def chain_recv(r):
-        @pl.when(z - 1 - r >= 0)
-        def _():
-            settle(wbuf.at[0], up_recv.at[r])
-            to_side(z - 1 - r)
-
-        @pl.when(z + 1 + r <= chips - 1)
-        def _():
-            settle(wbuf.at[0], down_recv.at[r])
-            to_side(z + 1 + r)
-
-    to_side(z)
-    chain_send(0)
     for r in range(1, chips - 1):
         if r < chips - 2:
             chain_recv(r - 1)
@@ -420,10 +445,7 @@
     width = channels // stn
     beams, inputs_all = beam_weights.shape[1], beam_weights.shape[2]
     chips = stn // 2
-    wanted = (2 * station_map[:, None] + jnp.arange(2, dtype=jnp.int32)[None, :]).reshape(
-        stn, tm, halves, rows
-    ).transpose(2, 1, 0, 3).reshape(1, inputs_all)
-    flags = jnp.repeat(station_flags, 2).astype(jnp.float32).reshape(1, inputs_all)
+    stations = station_map.shape[0]
     dma = pltpu.SemaphoreType.DMA
     vmem = pl.BlockSpec(memory_space=pltpu.VMEM)
     hbm = pl.BlockSpec(memory_space=pl.ANY)
@@ -449,8 +471,49 @@
         ],
         compiler_params=pltpu.CompilerParams(collective_id=0, has_side_effects=True),
     )(
-        voltages.reshape(2, tm, few, channels), beam_weights, wanted, flags, filter_taps, *tables(channels)
+        voltages.reshape(2, tm, few, channels), beam_weights, station_map.reshape(1, stations),
+        station_flags.reshape(1, stations), filter_taps, *tables(channels),
     )
+
+
+def order_kernel(p_ref, o_ref, rows_ref):
+    stn, beams, width = p_ref.shape
+    radix = o_ref.shape[1]
+    per_group = width // LANES
+    cuts = LANES // radix
+    for source in range(stn):
+        for kk in range(per_group):
+            rows_ref[pl.ds(source * per_group + kk, beams, stride=radix), :] = p_ref[
+                source, :, kk * LANES : (kk + 1) * LANES
+            ].astype(jnp.float32)
+    row = lax.broadcasted_iota(jnp.int32, (LANES, LANES), 0)
+    lane = lax.broadcasted_iota(jnp.int32, (LANES, LANES), 1)
+    chosen = lax.rem(row, radix) * cuts + lax.div(row, radix)
+    pick = jnp.where(lane == chosen, 1.0, 0.0).astype(jnp.bfloat16)
+    turned = lax.dot_general(
+        pick, rows_ref[...].astype(jnp.bfloat16), (((1,), (1,)), ((), ())), preferred_element_type=jnp.float32
+    )
+    place = lax.div(lax.broadcasted_iota(jnp.int32, (radix, LANES), 1), radix)
+    for tile in range(beams * radix // LANES):
+        parts = [turned[j * radix : (j + 1) * radix, tile * LANES : (tile + 1) * LANES] for j in range(cuts)]
+        for bb in range(cuts):
+            out = None
+            for j in range(cuts):
+                shift = (j - bb) % cuts * radix
+                moved = pltpu.roll(parts[j], shift, 1) if shift else parts[j]
+                out = moved if out is None else jnp.where(place == j, moved, out)
+            o_ref[tile * cuts + bb] = out
+
+
+def put_in_order(mine, radix):
+    stn, beams, _ = mine.shape
+    return pl.pallas_call(
+        order_kernel,
+        out_shape=jax.ShapeDtypeStruct((beams, radix, LANES), jnp.float32),
+        in_specs=[pl.BlockSpec(memory_space=pltpu.VMEM)],
+        out_specs=pl.BlockSpec(memory_space=pltpu.VMEM),
+        scratch_shapes=[pltpu.VMEM((beams * radix, LANES), jnp.float32)],
+    )(mine)
 
 
 def on_device(tm_size, stn_size, voltages, filter_taps, beam_weights, station_map, station_flags):
@@ -458,7 +521,7 @@
     few = voltages.shape[1] // tm_size
     if few % 32 == 0 and stn_size % 2 == 0:
         mine = fused(tm_size, stn_size, voltages, filter_taps, beam_weights, station_map, station_flags)
-        beams = mine.shape[1]
+        return put_in_order(mine, channels // LANES).reshape(mine.shape[1], 1, channels)
     else:
         weights = local_weights(beam_weights, station_map, station_flags, tm_size, stn_size)
         weight_all = lax.all_gather(weights, "stn", axis=1, tiled=True)

time: 90.2 us -> 85.1 us (0.943)
  local copies, waits for them, and re-layouts: 7.03 us -> 0 us
  Pallas kernels: 81.4 us -> 84.9 us
  other arithmetic: 1.44 us -> 0 us
    reshape x4 -> x0, local copies, waits for them, and re-layouts: 5.75 us -> none  [the longest x3 5.06 us: on_device(): return mine.transpose(1, 3, 0, 2).reshape(beams, 1, channels)]
    pallas_call x0 -> x1, Pallas kernels: none -> 3.46 us  [put_in_order(): pl.pallas_call(order_kernel, out_shape=jax.ShapeDtypeStruct((beams, radix...]
where the time goes in v3:
time: 85.1 us; the launch traced here: 84.9 us
  Pallas kernels  84.9 us (100%)
    pallas_call x1, Pallas kernels, fused(): pl.pallas_call(functools.partial(fused_kernel, tm, stn, radix, 1.0 / inpu...  81.4 us
    pallas_call x1, Pallas kernels, put_in_order(): pl.pallas_call(order_kernel, out_shape=jax.ShapeDtypeStruct((beams, radix...  3.46 us

profile of v3, /device:TPU:0, one launch (start us, length us, event | category | flops | bytes accessed | tf_op | source)
XLA Modules:
  0.0 84.9 jit_solution(7776379452054780258)
XLA Ops:
  0.0 81.4 %shard_map.91.p_ref = bf16[8,64,512]{2,1,0:T(8,128)(2,1)} custom-call(bf16[2,4,32,4096]{3,2,1,0:T(8,128)(2,1)} %bitcast.4, s32[2,64,1024]{2,1,0:T(8,128)} %w_ref.1, s32[1,512]{1,0:T(1,128)} %bitcast.5, s32[1,512]{1,0:T(1,128)} %bitcast.6, f32[12,4096]{1,0:T(8,128)} %taps_ref.1, f32[32,128]{1,0:T(8,128)} %constant.8.clone.twr_ref, ...), custom_call_target="tpu_custom_call" | custom-call | tf_op jit(solution)/shard_map/pallas_call | solution.py:453
  81.4 3.5 %shard_map.92 = f32[64,32,128]{2,1,0:T(8,128)} custom-call(bf16[8,64,512]{2,1,0:T(8,128)(2,1)} %shard_map.91.p_ref), custom_call_target="tpu_custom_call" | custom-call | tf_op jit(solution)/shard_map/pallas_call | solution.py:510

commit v4 on v3

--- a/solution.py
+++ b/solution.py
@@ -440,7 +440,7 @@
     channels = filter_taps.shape[1]
     radix = channels // LANES
     few = voltages.shape[1] // tm
-    halves = 2
+    halves = 4
     rows = few // halves
     width = channels // stn
     beams, inputs_all = beam_weights.shape[1], beam_weights.shape[2]

time: 85.1 us -> 84.3 us (level)
  no operation moved by 1% of the time
where the time goes in v4:
time: 84.3 us; the launch traced here: 84.1 us
  Pallas kernels  84.1 us (100%)
    pallas_call x1, Pallas kernels, fused(): pl.pallas_call(functools.partial(fused_kernel, tm, stn, radix, 1.0 / inpu...  80.6 us
    pallas_call x1, Pallas kernels, put_in_order(): pl.pallas_call(order_kernel, out_shape=jax.ShapeDtypeStruct((beams, radix...  3.46 us

profile of v4, /device:TPU:0, one launch (start us, length us, event | category | flops | bytes accessed | tf_op | source)
XLA Modules:
  0.0 84.1 jit_solution(15700611369011411786)
XLA Ops:
  0.0 80.6 %shard_map.91.p_ref = bf16[8,64,512]{2,1,0:T(8,128)(2,1)} custom-call(bf16[2,4,32,4096]{3,2,1,0:T(8,128)(2,1)} %bitcast.4, s32[2,64,1024]{2,1,0:T(8,128)} %w_ref.1, s32[1,512]{1,0:T(1,128)} %bitcast.5, s32[1,512]{1,0:T(1,128)} %bitcast.6, f32[12,4096]{1,0:T(8,128)} %taps_ref.1, f32[32,128]{1,0:T(8,128)} %constant.8.clone.twr_ref, ...), custom_call_target="tpu_custom_call" | custom-call | tf_op jit(solution)/shard_map/pallas_call | solution.py:453
  80.6 3.5 %shard_map.92 = f32[64,32,128]{2,1,0:T(8,128)} custom-call(bf16[8,64,512]{2,1,0:T(8,128)(2,1)} %shard_map.91.p_ref), custom_call_target="tpu_custom_call" | custom-call | tf_op jit(solution)/shard_map/pallas_call | solution.py:510
